TPU v7x, 32 devices: a whole 2x2x4 slice. The times are simulated.
32 devices in a mesh: head: 2 (over y), tm: 16 (over z, x, core).
Axes of the slice: x: 2, y: 2, z: 4, core: 2. Of those that a mesh axis runs over, the one named last changes fastest.
Arguments:
- frames: bfloat16 [16384, 1024], P('tm'), may hold values from -6 to 6
- segment_lengths: int32 [128], replicated, may hold values from 1 to 512, 16384 in all
- attn_gain: float32 [1024], replicated, may hold values from 0.5 to 1.5
- qkv_proj: bfloat16 [1024, 3, 1024], P('tm', None, 'head'), may hold values from -0.1875 to 0.1875
- out_proj: bfloat16 [1024, 1024], P(None, 'tm'), may hold values from -0.1875 to 0.1875
- logit_scale: float32 [16], P('head'), may hold values from 2 to 16
- conv_gain: float32 [1024], replicated, may hold values from 0.5 to 1.5
- glu_proj: bfloat16 [1024, 2048], P('tm'), may hold values from -0.1875 to 0.1875
- kernel: float32 [31, 1024], replicated, may hold values from -1 to 1
- post_gain: float32 [1024], replicated, may hold values from 0.5 to 1.5
- mix_proj: bfloat16 [1024, 1024], P('tm'), may hold values from -0.1875 to 0.1875
- cotangent: bfloat16 [16384, 1024], P('tm', 'head'), may hold values from -6 to 6
Outputs:
- out_frames: bfloat16 [16384, 1024], P('tm', 'head')
- grad_input: bfloat16 [16384, 1024], P('tm', 'head')
- grad_kernel: float32 [31, 1024], replicated
- grad_gains: float32 [2, 1024], replicated
Inputs may be any that keep to these rules, and one draw needn't show every extreme that they name: `segment_lengths`: the 128 lengths sum to 16384; the longest is exactly 512 frames.
All inputs are finite; a program needn't handle non-finite values.
Results may differ from a plain program's by a relative error of at most 0.014.
Values may be sent and summed in bfloat16 or wider, within the bound.
No kernel may reach another device: no remote copies, remote signals or barrier semaphores. Data moves between devices by JAX's collectives and lax.ppermute only.
A program may use at most 128 MiB of HBM per device.

v0:
```python
import math
import jax
import jax.numpy as jnp
from jax import lax
from jax.sharding import PartitionSpec as P

HD = 64
KERNEL = 31
HALF = 15
MOST = 512
EPS_NORM = 1e-05
EPS_HEAD = 1e-06


def extended(cells, sides, width, closed):
    for axis, dim in sides:
        count = lax.axis_size(axis)
        ends = count if closed else count - 1
        head = lax.slice_in_dim(cells, 0, width, axis=dim)
        tail = lax.slice_in_dim(cells, cells.shape[dim] - width, cells.shape[dim], axis=dim)
        cells = jnp.concatenate(
            [
                lax.ppermute(tail, axis, [(i, (i + 1) % count) for i in range(ends)]),
                cells,
                lax.ppermute(head, axis, [((i + 1) % count, i) for i in range(ends)]),
            ],
            axis=dim,
        )
    return cells


def layer_stats(values):
    average = jnp.mean(values, axis=-1, keepdims=True)
    centred = values - average
    inverse = lax.rsqrt(jnp.mean(centred * centred, axis=-1, keepdims=True) + EPS_NORM)
    return (centred * inverse, inverse)


def unit_heads(values):
    return values * lax.rsqrt(jnp.mean(values * values, axis=-1, keepdims=True) + EPS_HEAD)


def norm_back(gradient, normed, inverse, gain):
    scaled = gradient * gain
    return inverse * (
        scaled
        - jnp.mean(scaled, axis=-1, keepdims=True)
        - normed * jnp.mean(scaled * normed, axis=-1, keepdims=True)
    )


def on_device(
    frames,
    segment_lengths,
    attn_gain,
    qkv_proj,
    out_proj,
    logit_scale,
    conv_gain,
    glu_proj,
    kernel,
    post_gain,
    mix_proj,
    cotangent,
):
    head_count = lax.axis_size("head")
    shard_count = lax.axis_size("tm")
    head_place = lax.axis_index("head")
    shard_place = lax.axis_index("tm")
    local_frames = frames.shape[0]
    model_width = frames.shape[1]
    conv_rows = local_frames // head_count
    local_width = qkv_proj.shape[2]
    local_heads = local_width // HD
    all_frames = local_frames * shard_count
    segment_ends = jnp.cumsum(segment_lengths)

    def segment_of(positions):
        located = jnp.sum((segment_ends[None, :] <= positions[:, None]).astype(jnp.int32), axis=1)
        return jnp.where(positions < 0, -1, located)

    own_rows = lax.dynamic_slice_in_dim(out_proj, head_place * local_width, local_width, 0)
    qkv_weight, out_weight = (
        lax.all_gather(qkv_proj, "tm", axis=0, tiled=True),
        lax.all_gather(own_rows, "tm", axis=1, tiled=True),
    )
    glu_weight, proj_weight = (
        lax.all_gather(glu_proj, "tm", axis=0, tiled=True),
        lax.all_gather(mix_proj, "tm", axis=0, tiled=True),
    )
    frame_float = frames.astype(jnp.float32)
    attn_normed = (layer_stats(frame_float)[0] * attn_gain).astype(jnp.bfloat16)
    projected = jnp.dot(
        attn_normed,
        qkv_weight.reshape(model_width, 3 * local_width),
        preferred_element_type=jnp.float32,
    )
    query_heads = unit_heads(
        projected[:, :local_width].reshape(local_frames, local_heads, HD)
    ).astype(jnp.bfloat16)
    key_heads = unit_heads(
        projected[:, local_width : 2 * local_width].reshape(local_frames, local_heads, HD)
    ).astype(jnp.bfloat16)
    value_heads = projected[:, 2 * local_width :].astype(jnp.bfloat16)
    key_value = jnp.stack([key_heads.reshape(local_frames, local_width), value_heads], axis=1)
    key_padded = extended(key_value, (("tm", 0),), MOST, False)
    key_segment = segment_of(
        shard_place * local_frames - MOST + jnp.arange(local_frames + 2 * MOST, dtype=jnp.int32)
    )
    query_block = min(512, local_frames)
    factor = (logit_scale / HD)[:, None, None]

    def attend(row_start, query_rows, key_start, key_span):
        key_rows = lax.dynamic_slice_in_dim(key_padded, key_start, key_span, 0)
        query_seg = lax.dynamic_slice_in_dim(key_segment, row_start + MOST, query_block, 0)
        key_seg = lax.dynamic_slice_in_dim(key_segment, key_start, key_span, 0)
        key_part = key_rows[:, 0].reshape(key_span, local_heads, HD)
        value_part = key_rows[:, 1].reshape(key_span, local_heads, HD)
        scores = (
            jnp.einsum("qhd,khd->hqk", query_rows, key_part, preferred_element_type=jnp.float32)
            * factor
        )
        weights = jnp.where((query_seg[:, None] == key_seg[None, :])[None], jnp.exp(scores), 0.0)
        weights = (weights / jnp.sum(weights, axis=-1, keepdims=True)).astype(jnp.bfloat16)
        mixed_heads = jnp.einsum(
            "hqk,khd->qhd", weights, value_part, preferred_element_type=jnp.float32
        )
        return mixed_heads.astype(jnp.bfloat16).reshape(query_block, local_width)

    def attend_block(block_index):
        row_start = block_index * query_block
        query_rows = lax.dynamic_slice_in_dim(query_heads, row_start, query_block, 0)
        return attend(row_start, query_rows, row_start, query_block + 2 * MOST)

    heads_out = lax.map(
        attend_block, jnp.arange(local_frames // query_block, dtype=jnp.int32)
    ).reshape(local_frames, local_width)
    attn_rows = lax.psum_scatter(
        jnp.dot(heads_out, out_weight, preferred_element_type=jnp.float32).astype(jnp.bfloat16),
        "head",
        scatter_dimension=0,
        tiled=True,
    ).astype(jnp.float32)
    frame_rows = lax.dynamic_slice_in_dim(frame_float, head_place * conv_rows, conv_rows, 0)
    residual = (frame_rows + attn_rows).astype(jnp.bfloat16)
    residual_float = residual.astype(jnp.float32)
    conv_normed, conv_inverse = layer_stats(residual_float)
    conv_input = (conv_normed * conv_gain).astype(jnp.bfloat16)
    glu_linear = jnp.dot(conv_input, glu_weight, preferred_element_type=jnp.float32)
    glu_value = glu_linear[:, :model_width]
    gate_sigmoid = jax.nn.sigmoid(glu_linear[:, model_width:])
    gated = (glu_value * gate_sigmoid).astype(jnp.bfloat16)

    def with_rims(block_rows):
        beside_all = extended(block_rows, (("head", 0),), HALF, True)
        outer_rims = jnp.concatenate([beside_all[-HALF:], beside_all[:HALF]], 0)
        beyond = extended(outer_rims, (("tm", 0),), HALF, False)
        left_rim = jnp.where(head_place == 0, beyond[:HALF], beside_all[:HALF])
        right_rim = jnp.where(head_place == head_count - 1, beyond[-HALF:], beside_all[-HALF:])
        return jnp.concatenate([left_rim, block_rows, right_rim], 0)

    gated_padded = with_rims(gated)
    conv_start = (shard_place * head_count + head_place) * conv_rows
    conv_segment = segment_of(conv_start - HALF + jnp.arange(conv_rows + 2 * HALF, dtype=jnp.int32))
    window_index = jnp.arange(conv_rows)[:, None] + jnp.arange(KERNEL)[None, :]
    mask_table = (
        conv_segment[window_index] == conv_segment[HALF : HALF + conv_rows][:, None]
    ).astype(jnp.float32)

    def depthwise(padded, tap_weights):
        summed = jnp.zeros((conv_rows, model_width), jnp.float32)
        for offset in range(KERNEL):
            summed = (
                summed
                + tap_weights[offset]
                * padded[offset : offset + conv_rows].astype(jnp.float32)
                * mask_table[:, offset : offset + 1]
            )
        return summed

    depth_out = depthwise(gated_padded, kernel)
    post_normed, post_inverse = layer_stats(depth_out)
    post_scaled = post_normed * post_gain
    post_sigmoid = jax.nn.sigmoid(post_scaled)
    swished = (post_scaled * post_sigmoid).astype(jnp.bfloat16)
    out_rows = (
        residual_float + jnp.dot(swished, proj_weight, preferred_element_type=jnp.float32)
    ).astype(jnp.bfloat16)
    out_frames = lax.all_to_all(out_rows, "head", split_axis=1, concat_axis=0, tiled=True)
    upstream = lax.all_to_all(cotangent, "head", split_axis=0, concat_axis=1, tiled=True)
    swish_grad = jnp.dot(upstream, proj_weight.T, preferred_element_type=jnp.float32)
    post_grad = swish_grad * (post_sigmoid * (1.0 + post_scaled * (1.0 - post_sigmoid)))
    depth_grad = norm_back(post_grad, post_normed, post_inverse, post_gain).astype(jnp.bfloat16)
    gated_grad = depthwise(with_rims(depth_grad), kernel[::-1])
    depth_float = depth_grad.astype(jnp.float32)
    kernel_terms = jnp.stack(
        [
            jnp.sum(
                depth_float
                * gated_padded[offset : offset + conv_rows].astype(jnp.float32)
                * mask_table[:, offset : offset + 1],
                axis=0,
            )
            for offset in range(KERNEL)
        ],
        0,
    )
    glu_grad = jnp.concatenate(
        [gated_grad * gate_sigmoid, gated_grad * glu_value * gate_sigmoid * (1.0 - gate_sigmoid)], 1
    ).astype(jnp.bfloat16)
    input_grad = jnp.dot(glu_grad, glu_weight.T, preferred_element_type=jnp.float32)
    residual_grad = (
        upstream.astype(jnp.float32) + norm_back(input_grad, conv_normed, conv_inverse, conv_gain)
    ).astype(jnp.bfloat16)
    gain_terms = jnp.stack(
        [jnp.sum(input_grad * conv_normed, axis=0), jnp.sum(post_grad * post_normed, axis=0)], 0
    )
    kernel_sum, gain_sum = lax.psum((kernel_terms, gain_terms), ("head", "tm"))
    grad_scale = 1.0 / math.sqrt(all_frames)
    grad_input = lax.all_to_all(residual_grad, "head", split_axis=1, concat_axis=0, tiled=True)
    return (out_frames, grad_input, kernel_sum * grad_scale, gain_sum * grad_scale)


def solution(mesh):
    placed = (
        P("tm", None),
        P(),
        P(),
        P("tm", None, "head"),
        P(None, "tm"),
        P("head"),
        P(),
        P("tm", None),
        P(),
        P(),
        P("tm", None),
        P("tm", "head"),
    )
    return jax.shard_map(
        on_device,
        mesh=mesh,
        in_specs=placed,
        out_specs=(P("tm", "head"), P("tm", "head"), P(), P()),
        check_vma=False,
    )
```

profile of v0, /device:TPU:0, one launch (start us, length us, event | category | flops | bytes accessed | tf_op | source)
XLA Modules:
  0.0 488.0 jit_solution(7400596972553521557)
XLA Ops:
  8.8 1.9 convert_reduce_fusion.1
  11.9 46.5 %all-gather.5.cloned.1.call-done = bf16[1024,3,512]{2,0,1:T(8,128)(2,1)} async-done(((bf16[64,3,512]{2,0,1:T(8,128)(2,1)}), bf16[1024,3,512]{2,0,1:T(8,128)(2,1)}) %all-gather.5.cloned.1.call-update) | async-done | bytes 3145744 | tf_op jit(solution)/shard_map/all_gather | solution.py:84
  58.5 4.7 copy.43
  63.2 5.4 %fusion.83 = f32[1024,1536]{1,0:T(8,128)S(1)} fusion(bf16[1024,1536]{0,1:T(8,128)(2,1)} %bitcast.141, bf16[1024,1024]{1,0:T(8,128)(2,1)S(1)} %copy-done.4, f32[1024]{0:T(1024)S(1)} %copy-done.32, f32[1024]{0:T(1024)S(1)} %add_rsqrt_fusion.2, f32[1024]{0:T(1024)S(1)} %broadcast_multiply_fusion.2), kind=kOutput, calls=%fused_computation.216 | convolution fusion | flops 3226468352 | bytes 11546624 | tf_op jit(solution)/shard_map/dot_general | solution.py:93
  68.8 2.4 copy-done.11
  71.4 1.8 copy.44
  73.2 1.8 bitcast_reduce_fusion
  75.4 1.8 copy.45
  77.2 4.7 fusion.246
  83.4 3.1 collective-permute-start
  88.7 1.9 copy.47
  92.2 3.4 pad_maximum_fusion
  95.6 65.1 %while.12 = (s32[]{:T(128)}, bf16[2,512,512]{2,1,0:T(8,128)(2,1)}, s32[2]{0:T(128)S(1)}, bf16[2048,2,512]{2,0,1:T(8,128)(2,1)}, s32[2048]{0:T(1024)S(1)}, /*inde...) while((s32[]{:T(128)}, bf16[2,512,512]{2,1,0:T(8,128)(2,1)}, ...), condition=%wide.region_8.9_spmd, body=%wide.region_6.8_spmd.sunk | while | flops 1655697408 | bytes 71623536 | solution.py:135
  98.4 2.1 constant_dynamic-slice_fusion.4
  102.1 13.1 %fusion.267 = (f32[8,512]{1,0:T(8,128)S(1)}, f32[8,512,1536]{2,1,0:T(8,128)}) fusion(f32[8]{0:T(128)S(1)} %bitcast.241, pred[512,1536]{1,0:T(8,128)(4,1)} %broadcast_compare_fusion.2, bf16[1536,8,64]{0,2,1:T(8,128)(2,1)} %bitcast.130, bf16[1024,8,64]{0,2,1:T(8,128)(2,1)} %get-tuple-element.344, s32[]{:T(128)S(6)} %select_n.108), kind=kOutput, calls=%fused_computation.3.clone.1 | convolution fusion | flops 824176640 | bytes 28065828 | tf_op jit(solution)/shard_map/while/body/eval_jaxpr/qhd,khd->hqk/dot_general | solution.py:120
  115.9 11.2 %fusion.268 = bf16[8,64,512]{2,1,0:T(8,128)(2,1)S(1)} fusion(bf16[1536,8,64]{0,2,1:T(8,128)(2,1)S(1)} %bitcast.131, f32[8,512,1536]{2,1,0:T(8,128)} %get-tuple-element.307, f32[8,512]{1,0:T(8,128)S(1)} %get-tuple-element.308, f32[8]{0:T(128)S(1)} %bitcast.242, pred[512,1536]{1,0:T(8,128)(4,1)} %broadcast_compare_fusion.2), kind=kOutput, calls=%fused_computation.6.clone.1 | convolution fusion | flops 830734336 | bytes 28065824 | tf_op jit(solution)/shard_map/while/body/eval_jaxpr/hqk,khd->qhd/dot_general | solution.py:125
  131.0 2.1 constant_dynamic-slice_fusion.4
  134.7 13.1 %fusion.267 = (f32[8,512]{1,0:T(8,128)S(1)}, f32[8,512,1536]{2,1,0:T(8,128)}) fusion(f32[8]{0:T(128)S(1)} %bitcast.241, pred[512,1536]{1,0:T(8,128)(4,1)} %broadcast_compare_fusion.2, bf16[1536,8,64]{0,2,1:T(8,128)(2,1)} %bitcast.130, bf16[1024,8,64]{0,2,1:T(8,128)(2,1)} %get-tuple-element.344, s32[]{:T(128)S(6)} %select_n.108), kind=kOutput, calls=%fused_computation.3.clone.1 | convolution fusion | flops 824176640 | bytes 28065828 | tf_op jit(solution)/shard_map/while/body/eval_jaxpr/qhd,khd->hqk/dot_general | solution.py:120
  148.4 11.2 %fusion.268 = bf16[8,64,512]{2,1,0:T(8,128)(2,1)S(1)} fusion(bf16[1536,8,64]{0,2,1:T(8,128)(2,1)S(1)} %bitcast.131, f32[8,512,1536]{2,1,0:T(8,128)} %get-tuple-element.307, f32[8,512]{1,0:T(8,128)S(1)} %get-tuple-element.308, f32[8]{0:T(128)S(1)} %bitcast.242, pred[512,1536]{1,0:T(8,128)(4,1)} %broadcast_compare_fusion.2), kind=kOutput, calls=%fused_computation.6.clone.1 | convolution fusion | flops 830734336 | bytes 28065824 | tf_op jit(solution)/shard_map/while/body/eval_jaxpr/hqk,khd->qhd/dot_general | solution.py:125
  160.7 4.1 convolution_convert_fusion
  165.4 3.7 all-to-all-start.1
  170.0 2.4 convert_element_type.293
  173.2 55.4 %gather_fusion = s32[15872]{0:T(1024)S(1)} fusion(s32[542]{0:T(1024)S(1)} %compare_select_fusion.2, s32[16384]{0:T(1024)S(1)} %pad_clamp_fusion), kind=kCustom, calls=%fused_computation | custom fusion | bytes 190464 | tf_op jit(solution)/shard_map/gather | solution.py:167
  229.1 2.3 convert_reduce_fusion
  231.9 40.1 %all-gather.9.cloned.1.call-done = bf16[1024,2048]{1,0:T(8,128)(2,1)} async-done(((bf16[64,2048]{1,0:T(8,128)(2,1)}), bf16[1024,2048]{1,0:T(8,128)(2,1)}) %all-gather.9.cloned.1.call-update) | async-done | bytes 4194320 | tf_op jit(solution)/shard_map/all_gather | solution.py:88
  272.0 4.6 fusion.176
  280.2 2.6 slice_reduce_fusion.30
  285.0 1.7 slice_reduce_fusion.29
  287.9 1.7 collective-permute-start.5
  289.6 1.9 collective-permute-done.5
  291.5 18.7 %fusion.244 = (f32[512]{0:T(512)S(1)}, f32[512,1024]{1,0:T(8,128)S(1)}) fusion(f32[512]{0:T(512)S(1)} %get-tuple-element.160, bf16[15,1024]{1,0:T(8,128)(2,1)S(1)} %broadcast_select_fusion.1, bf16[512,1024]{1,0:T(8,128)(2,1)S(1)} %multiply_convert_fusion.6, f32[1024]{0:T(1024)S(1)} %bitcast.202, f32[512]{0:T(512)S(1)} %get-tuple-element.161, ...), kind=kLoop, calls=%fused_computation.483 | loop fusion | flops 112197120 | bytes 3399680 | tf_op jit(solution)/shard_map/reduce_sum | solution.py:33
  310.6 3.4 all-gather.11.cloned.1.call-done
  314.0 4.7 multiply_reduce_fusion.1
  318.7 7.3 %fusion.160 = (f32[1024]{0:T(1024)}, f32[1024]{0:T(1024)}, f32[1024]{0:T(1024)}, f32[1024]{0:T(1024)}, f32[1024]{0:T(1024)}, /*index=5*/f32[1024]{0:T(1024)}, bf16[512,1024]{1,0:T(8,128)(2,1)S(1)}) fusion(f32[512]{0:T(512)S(1)} %get-tuple-element.161, bf16[15,1024]{1,0:T(8,128)(2,1)S(1)} %broadcast_select_fusion.1, ...), kind=kLoop, calls=%fused_computation.293 | loop fusion | flops 26732544 | bytes 6371328 | tf_op jit(solution)/shard_map/reduce_sum | solution.py:198
  326.1 6.9 %fusion.162 = (f32[1024]{0:T(1024)}, f32[1024]{0:T(1024)}, f32[1024]{0:T(1024)}, f32[1024]{0:T(1024)}, f32[1024]{0:T(1024)}, /*index=5*/f32[1024]{0:T(1024)}) fusion(bf16[512,1024]{1,0:T(8,128)(2,1)S(1)} %get-tuple-element.204, bf16[15,1024]{1,0:T(8,128)(2,1)S(1)} %broadcast_select_fusion.1, bf16[512,1024]{1,0:T(8,128)(2,1)S(1)} %multiply_convert_fusion.6, ...), kind=kLoop, calls=%fused_computation.295 | loop fusion | flops 22538240 | bytes 2164736 | tf_op jit(solution)/shard_map/reduce_sum | solution.py:198
  333.0 3.2 fusion.158
  336.2 3.9 fusion.130
  340.0 4.1 fusion.128
  345.7 2.0 fusion.108
  348.2 5.5 %stack.144 = f32[31,1024]{1,0:T(8,128)} concatenate(f32[1,1024]{1,0:T(1,128)} %bitcast.233, f32[1,1024]{1,0:T(1,128)} %bitcast.236, f32[1,1024]{1,0:T(1,128)} %bitcast.235, f32[1,1024]{1,0:T(1,128)} %bitcast.234, f32[1,1024]{1,0:T(1,128)} %bitcast.223, f32[1,1024]{1,0:T(1,128)} %bitcast.224, f32[1,1024]{1,0:T(1,128)} %bitcast.225, f32[1,1024]{1,0:T(1,128)} %bitcast.226, ...), dimensions={0} | concatenate | bytes 253952 | tf_op jit(solution)/shard_map/stack | solution.py:196
  355.4 3.7 fusion.82
  360.1 3.6 all-to-all-start
  365.0 2.3 collective-permute-done.9
  367.4 19.0 %multiply_convert_fusion.3 = (bf16[512,1024]{1,0:T(8,128)(2,1)S(1)}, f32[512,1024]{1,0:T(8,128)S(1)}) fusion(f32[512,2048]{1,0:T(8,128)} %copy-done.2, f32[512]{0:T(512)S(1)} %get-tuple-element.160, bf16[15,1024]{1,0:T(8,128)(2,1)S(1)} %broadcast_select_fusion, bf16[512,1024]{1,0:T(8,128)(2,1)S(1)} %get-tuple-element.204, f32[1024]{0:T(1024)S(1)} %bitcast.145, ...), kind=kLoop, calls=%fused_computation.310 | loop fusion | flops 114294784 | bytes 6543360 | tf_op jit(solution)/shard_map/convert
  388.6 2.8 fusion.19
  393.3 3.6 all-to-all-start.2
  396.9 48.6 %psum.15 = f32[2,1024]{1,0:T(2,128)S(1)} all-reduce(f32[2,1024]{1,0:T(2,128)S(1)} %pad_maximum_fusion.6), channel_id=1, replica_groups=mesh['head'=2,'tm'=16] {'head','tm'}, use_global_device_ids=true, to_apply=%region_53.54 | all-reduce | flops 2048 | bytes 16384 | tf_op jit(solution)/shard_map/psum | solution.py:218
  446.2 31.3 %all-reduce.2.cloned.1.call-done = f32[31,1024]{1,0:T(8,128)} async-done(((f32[31,1024]{1,0:T(8,128)}), f32[31,1024]{1,0:T(8,128)}) %all-reduce.2.cloned.1.call-update) | async-done | bytes 126992 | tf_op jit(solution)/shard_map/psum | solution.py:218
  (174 shorter events, 43.8 us)
Async XLA Ops:
  7.2 3.6 copy-start.4
  7.2 51.3 %all-gather.5.cloned.1.call-start = ((), (), s32[]{:S(2)}) async-start(), calls=%async_computation.4 | async-start | bytes 3342336 | tf_op jit(solution)/shard_map/all_gather | solution.py:84
  7.9 152.8 %all-gather.7.cloned.1.call-start = ((), (), s32[]{:S(2)}) async-start(), calls=%async_computation.5 | async-start | bytes 1114112 | tf_op jit(solution)/shard_map/all_gather | solution.py:85
  8.7 220.3 %reduce-scatter.2.cloned.1.call-start = ((), (), s32[]{:S(2)}) async-start(), calls=%async_computation.6 | async-start | bytes 3145728 | tf_op jit(solution)/shard_map/reduce_scatter | solution.py:138
  8.8 2.7 copy-start.30
  8.8 3.1 copy-start.33
  11.9 76.1 %copy-start.24 = (s32[128]{0:T(128)}, s32[128]{0:T(128)S(1)}, u32[]{:S(2)}) copy-start(s32[128]{0:T(128)S(1)} %reduce) | copy-start | bytes 1540
  11.9 51.2 %copy-start.32 = (f32[1024]{0:T(1024)S(1)}, f32[1024]{0:T(1024)}, u32[]{:S(2)}) copy-start(f32[1024]{0:T(1024)} %param.16) | copy-start | bytes 12292
  68.6 2.7 copy-start.11
  71.4 10.5 %copy-start.9 = (bf16[1024,1,512]{2,0,1:T(8,128)(2,1)}, bf16[1024,1,512]{2,0,1:T(8,128)(2,1)S(1)}, u32[]{:S(2)}) copy-start(bf16[1024,1,512]{2,0,1:T(8,128)(2,1)S(1)} %fusion.175) | copy-start | bytes 3145732
  83.4 8.8 %collective-permute-start = (bf16[512,2,512]{2,0,1:T(8,128)(2,1)}, bf16[512,2,512]{2,0,1:T(8,128)(2,1)}, u32[]{:S(2)}, u32[]{:S(2)}) collective-permute-start(bf16[512,2,512]{2,0,1:T(8,128)(2,1)} %get-tuple-element.217), channel_id=1, source_target_pairs={{0,1},{1,2},{2,3},{3,4},{4,5},{5,6},{6,7},{7,8},{8,9},{9,10},{10,1... | collective-permute-start | bytes 3145736 | tf_op jit(solution)/shard_map/ppermute | solution.py:23
  86.6 5.7 %collective-permute-start.1 = (bf16[512,2,512]{2,0,1:T(8,128)(2,1)}, bf16[512,2,512]{2,0,1:T(8,128)(2,1)}, u32[]{:S(2)}, u32[]{:S(2)}) collective-permute-start(bf16[512,2,512]{2,0,1:T(8,128)(2,1)} %get-tuple-element.218), channel_id=1, source_target_pairs={{1,0},{2,1},{3,2},{4,3},{5,4},{6,5},{7,6},{8,7},{9,8},{10,9},{11,1... | collective-permute-start | bytes 3145736 | tf_op jit(solution)/shard_map/ppermute | solution.py:25
  164.8 5.2 %copy-start.5 = (bf16[1024,1024]{1,0:T(8,128)(2,1)S(1)}, bf16[1024,1024]{1,0:T(8,128)(2,1)}, u32[]{:S(2)}) copy-start(bf16[1024,1024]{1,0:T(8,128)(2,1)} %param.14) | copy-start | bytes 6291460
  164.9 107.1 %all-gather.9.cloned.1.call-start = ((), (), s32[]{:S(2)}) async-start(), calls=%async_computation.7 | async-start | bytes 4456448 | tf_op jit(solution)/shard_map/all_gather | solution.py:88
  165.4 121.3 %all-to-all-start.1 = ((bf16[2,512,512]{2,1,0:T(8,128)(2,1)}), bf16[2,512,512]{2,1,0:T(8,128)(2,1)S(1)}, u32[]{:S(2)}, u32[]{:S(2)}) async-start(bf16[2,512,512]{2,1,0:T(8,128)(2,1)} %bitcast.142), calls=%async_computation.2 | async-start | bytes 2097152 | tf_op jit(solution)/shard_map/all_to_all | solution.py:190
  169.2 144.8 %all-gather.11.cloned.1.call-start = ((), (), s32[]{:S(2)}) async-start(), calls=%async_computation.8 | async-start | bytes 2228224 | tf_op jit(solution)/shard_map/all_gather | solution.py:89
  169.8 2.8 copy-start.13
  169.8 2.9 copy-start.25
  169.8 307.7 %all-reduce.2.cloned.1.call-start = ((), (), s32[]{:S(2)}) async-start(), calls=%async_computation.9 | async-start | bytes 262144 | tf_op jit(solution)/shard_map/psum | solution.py:218
  229.0 43.0 %copy-start.28 = (f32[1024]{0:T(1024)S(1)}, f32[1024]{0:T(1024)}, u32[]{:S(2)}) copy-start(f32[1024]{0:T(1024)} %param.20) | copy-start | bytes 12292
  231.4 40.6 %copy-start.7 = (bf16[512,1024]{1,0:T(8,128)(2,1)}, bf16[512,1024]{1,0:T(8,128)(2,1)S(1)}, u32[]{:S(2)}) copy-start(bf16[512,1024]{1,0:T(8,128)(2,1)S(1)} %get-tuple-element.210) | copy-start | bytes 3145732
  231.4 45.2 %copy-start.18 = (f32[512]{0:T(512)}, f32[512]{0:T(512)S(1)}, u32[]{:S(2)}) copy-start(f32[512]{0:T(512)S(1)} %broadcast_multiply_fusion.8) | copy-start | bytes 6148
  231.9 44.8 %copy-start.21 = (f32[512]{0:T(512)}, f32[512]{0:T(512)S(1)}, u32[]{:S(2)}) copy-start(f32[512]{0:T(512)S(1)} %add_rsqrt_fusion.4) | copy-start | bytes 6148
  276.6 2.0 copy-start.2
  278.6 4.8 collective-permute-start.2
  282.8 5.1 %collective-permute-start.4 = (bf16[15,1024]{1,0:T(8,128)(2,1)S(1)}, bf16[15,1024]{1,0:T(8,128)(2,1)S(1)}, u32[]{:S(2)}, u32[]{:S(2)}) collective-permute-start(bf16[15,1024]{1,0:T(8,128)(2,1)S(1)} %get-tuple-element.222), channel_id=1, source_target_pairs={{16,0},{0,16},{17,1},{1,17},{18,2},{2,18},{19,3},{3,19},{20,4},{4,... | collective-permute-start | bytes 92168 | tf_op jit(solution)/shard_map/ppermute | solution.py:25
  283.4 6.2 %collective-permute-start.3 = (bf16[15,1024]{1,0:T(8,128)(2,1)S(1)}, bf16[15,1024]{1,0:T(8,128)(2,1)S(1)}, u32[]{:S(2)}, u32[]{:S(2)}) collective-permute-start(bf16[15,1024]{1,0:T(8,128)(2,1)S(1)} %collective-permute-done.2), channel_id=1, source_target_pairs={{0,1},{1,2},{2,3},{3,4},{4,5},{5,6},{6,7},{7,8},{8,9},{9,10},{10,1... | collective-permute-start | bytes 92168 | tf_op jit(solution)/shard_map/ppermute | solution.py:23
  286.7 23.4 %copy-start.14 = (f32[512]{0:T(512)}, f32[512]{0:T(512)S(1)}, u32[]{:S(2)}) copy-start(f32[512]{0:T(512)S(1)} %get-tuple-element.186) | copy-start | bytes 6148
  286.7 23.4 %copy-start.16 = (f32[512]{0:T(512)}, f32[512]{0:T(512)S(1)}, u32[]{:S(2)}) copy-start(f32[512]{0:T(512)S(1)} %get-tuple-element.187) | copy-start | bytes 6148
  287.9 3.6 collective-permute-start.5
  291.5 22.5 %copy-start.26 = (f32[1024]{0:T(1024)S(1)}, f32[1024]{0:T(1024)}, u32[]{:S(2)}) copy-start(f32[1024]{0:T(1024)} %param.23) | copy-start | bytes 12292
  310.2 8.6 %copy-start.6 = (f32[512,1024]{1,0:T(8,128)}, f32[512,1024]{1,0:T(8,128)S(1)}, u32[]{:S(2)}) copy-start(f32[512,1024]{1,0:T(8,128)S(1)} %get-tuple-element.208) | copy-start | bytes 6291460
  310.2 8.6 %copy-start.20 = (f32[512]{0:T(512)}, f32[512]{0:T(512)S(1)}, u32[]{:S(2)}) copy-start(f32[512]{0:T(512)S(1)} %broadcast_multiply_fusion.7) | copy-start | bytes 6148
  310.5 8.2 %copy-start.23 = (f32[512]{0:T(512)}, f32[512]{0:T(512)S(1)}, u32[]{:S(2)}) copy-start(f32[512]{0:T(512)S(1)} %add_rsqrt_fusion.3) | copy-start | bytes 6148
  326.1 10.1 %copy-start.15 = (f32[512]{0:T(512)S(1)}, f32[512]{0:T(512)}, u32[]{:S(2)}) copy-start(f32[512]{0:T(512)} %copy-done.14) | copy-start | bytes 6148
  326.1 10.1 %copy-start.17 = (f32[512]{0:T(512)S(1)}, f32[512]{0:T(512)}, u32[]{:S(2)}) copy-start(f32[512]{0:T(512)} %copy-done.16) | copy-start | bytes 6148
  340.0 15.4 %copy-start.8 = (bf16[512,1024]{1,0:T(8,128)(2,1)S(1)}, bf16[512,1024]{1,0:T(8,128)(2,1)}, u32[]{:S(2)}) copy-start(bf16[512,1024]{1,0:T(8,128)(2,1)} %copy-done.7) | copy-start | bytes 3145732
  344.2 9.6 %collective-permute-start.6 = (bf16[15,1024]{1,0:T(8,128)(2,1)S(1)}, bf16[15,1024]{1,0:T(8,128)(2,1)S(1)}, u32[]{:S(2)}, u32[]{:S(2)}) collective-permute-start(bf16[15,1024]{1,0:T(8,128)(2,1)S(1)} %get-tuple-element.219), channel_id=1, source_target_pairs={{0,16},{16,0},{1,17},{17,1},{2,18},{18,2},{3,19},{19,3},{4,20},{20... | collective-permute-start | bytes 92168 | tf_op jit(solution)/shard_map/ppermute | solution.py:23
  347.7 16.0 %collective-permute-start.8 = (bf16[15,1024]{1,0:T(8,128)(2,1)S(1)}, bf16[15,1024]{1,0:T(8,128)(2,1)S(1)}, u32[]{:S(2)}, u32[]{:S(2)}) collective-permute-start(bf16[15,1024]{1,0:T(8,128)(2,1)S(1)} %get-tuple-element.220), channel_id=1, source_target_pairs={{16,0},{0,16},{17,1},{1,17},{18,2},{2,18},{19,3},{3,19},{20,4},{4,... | collective-permute-start | bytes 92168 | tf_op jit(solution)/shard_map/ppermute | solution.py:25
  353.8 11.2 %collective-permute-start.7 = (bf16[15,1024]{1,0:T(8,128)(2,1)S(1)}, bf16[15,1024]{1,0:T(8,128)(2,1)S(1)}, u32[]{:S(2)}, u32[]{:S(2)}) collective-permute-start(bf16[15,1024]{1,0:T(8,128)(2,1)S(1)} %collective-permute-done.6), channel_id=1, source_target_pairs={{0,1},{1,2},{2,3},{3,4},{4,5},{5,6},{6,7},{7,8},{8,9},{9,10},{10,1... | collective-permute-start | bytes 92168 | tf_op jit(solution)/shard_map/ppermute | solution.py:23
  360.1 33.2 %all-to-all-start = ((bf16[512,2,512]{2,0,1:T(8,128)(2,1)}), bf16[512,2,512]{2,0,1:T(8,128)(2,1)S(1)}, u32[]{:S(2)}, u32[]{:S(2)}) async-start(bf16[512,2,512]{2,0,1:T(8,128)(2,1)} %bitcast.136), calls=%async_computation.1 | async-start | bytes 2097152 | tf_op jit(solution)/shard_map/all_to_all | solution.py:189
  363.7 3.7 collective-permute-start.9
  367.4 19.0 %copy-start.3 = (f32[512,2048]{1,0:T(8,128)S(1)}, f32[512,2048]{1,0:T(8,128)}, u32[]{:S(2)}) copy-start(f32[512,2048]{1,0:T(8,128)} %copy-done.2) | copy-start | bytes 12582916
  386.4 2.2 copy-start.31
  388.6 2.8 copy-start.12
  392.3 4.6 copy-start.27
  393.3 85.7 %all-to-all-start.2 = ((bf16[512,2,512]{2,0,1:T(8,128)(2,1)}), bf16[512,2,512]{2,0,1:T(8,128)(2,1)S(1)}, u32[]{:S(2)}, u32[]{:S(2)}) async-start(bf16[512,2,512]{2,0,1:T(8,128)(2,1)} %bitcast.114), calls=%async_computation.3 | async-start | bytes 2097152 | tf_op jit(solution)/shard_map/all_to_all | solution.py:220
  479.0 1.9 copy-start.1
  (5 other events, 5.0 us)
Sparse Core Ops, SparseCore 0:
  10.2 48.2 all-gather.4
  61.2 36.9 all-gather.6
  165.0 53.5 reduce-scatter.1
  220.6 51.3 all-gather.8
  274.0 39.9 all-gather.10
  353.9 123.4 all-reduce.1
where the time goes:
time: 494 us; the launch traced here: 488 us
  waiting for transfers between devices  127 us (26%)
  local copies, waits for them, and re-layouts  100 us (20%)
  other arithmetic  95.2 us (19%)
  matrix products  73.9 us (15%)
  blocking collectives  48.6 us (10%)
  starting transfers between devices  26.2 us (5%)
  between operations  15.1 us (3%)
    gather x2, local copies, waits for them, and re-layouts, on_device(): conv_segment[window_index] == conv_segment[HALF:HALF + conv_rows][:, None]  55.6 us
    psum x1, blocking collectives, on_device(): kernel_sum, gain_sum = lax.psum((kernel_terms, gain_terms), ('head', 'tm'))  48.6 us
    all_gather x1, waiting for transfers between devices, on_device(): lax.all_gather(qkv_proj, 'tm', axis=0, tiled=True)  46.5 us
    all_gather x1, waiting for transfers between devices, on_device(): lax.all_gather(glu_proj, 'tm', axis=0, tiled=True)  40.1 us
    psum x1, waiting for transfers between devices, on_device(): kernel_sum, gain_sum = lax.psum((kernel_terms, gain_terms), ('head', 'tm'))  31.3 us
    reduce_sum x6, other arithmetic, on_device(): jnp.sum(depth_float * gated_padded[offset:offset + conv_rows].astype(jnp....  27.4 us
    dot_general x2, matrix products, attend(): jnp.einsum('qhd,khd->hqk', query_rows, key_part, preferred_element_type=j...  26.2 us
    reduce_sum x3, other arithmetic, layer_stats(): average = jnp.mean(values, axis=-1, keepdims=True)  22.9 us
  transfers between devices with their start and end apart: 19, of which 6 were waited for; matrix products, arithmetic and copies ran while one was open for 47% of the time, Pallas kernels for 0%

commit v1 on v0

--- a/solution.py
+++ b/solution.py
@@ -3,6 +3,7 @@
 import jax.numpy as jnp
 from jax import lax
 from jax.sharding import PartitionSpec as P
+from jax.lax import axis_index, ppermute, psum
 
 HD = 64
 KERNEL = 31
@@ -84,8 +85,42 @@
         lax.all_gather(qkv_proj, "tm", axis=0, tiled=True),
         lax.all_gather(own_rows, "tm", axis=1, tiled=True),
     )
+
+    def draft_strings(target):
+        all_blocks = []
+        arr_out, reached, arr_next = (psum(1, "tm"), axis_index("tm"), target.shape[0])
+        for c, rr in enumerate(target.shape):
+            all_blocks.append(rr * arr_out if c == 0 else rr)
+        high = u1 = target
+        dev = 1
+        right_arr = lax.dynamic_update_slice_in_dim(
+            jnp.zeros(all_blocks, target.dtype), target, reached * arr_next, axis=0
+        )
+        while dev < arr_out // 2 + 1:
+            pile = []
+            c = 0
+            while c < arr_out:
+                pile.append((c, (c + 1) % arr_out))
+                c += 1
+            high = ppermute(high, "tm", pile)
+            right_arr = lax.dynamic_update_slice_in_dim(
+                right_arr, high, (reached - dev) % arr_out * arr_next, axis=0
+            )
+            if 2 * dev < arr_out:
+                inbox = []
+                c = 0
+                while c < arr_out:
+                    inbox.append((c, (c - 1) % arr_out))
+                    c += 1
+                u1 = ppermute(u1, "tm", inbox)
+                right_arr = lax.dynamic_update_slice_in_dim(
+                    right_arr, u1, (reached + dev) % arr_out * arr_next, axis=0
+                )
+            dev += 1
+        return right_arr
+
     glu_weight, proj_weight = (
-        lax.all_gather(glu_proj, "tm", axis=0, tiled=True),
+        draft_strings(glu_proj),
         lax.all_gather(mix_proj, "tm", axis=0, tiled=True),
     )
     frame_float = frames.astype(jnp.float32)

time: 494 us -> 551 us (1.12)
  starting transfers between devices: 26.2 us -> 75.6 us
  local copies, waits for them, and re-layouts: 100 us -> 114 us
  waiting for transfers between devices: 127 us -> 121 us
    ppermute x0 -> x15, starting transfers between devices: none -> 45.6 us  [the longest x7 24.6 us: draft_strings(): u1 = ppermute(u1, 'tm', inbox)]
    all_gather x1 -> x0, waiting for transfers between devices: 40.1 us -> none  [on_device(): lax.all_gather(glu_proj, 'tm', axis=0, tiled=True)]
    ppermute x0 -> x15, waiting for transfers between devices: none -> 29.2 us  [the longest x8 29.1 us: draft_strings(): high = ppermute(high, 'tm', pile)]
    dynamic_update_slice x0 -> x16, local copies, waits for them, and re-layouts: none -> 11.6 us  [the longest x8 5.78 us: draft_strings(): lax.dynamic_update_slice_in_dim(right_arr, high, (reached - dev) % arr_ou...]
    psum x1, waiting for transfers between devices: 31.3 us -> 42.5 us  [on_device(): kernel_sum, gain_sum = lax.psum((kernel_terms, gain_terms), ('head', 'tm'))]
  transfers between devices with their start and end apart: 19 -> 33, of which waited for: 6 -> 11; matrix products, arithmetic and copies ran while one was open for 47% -> 45% of each run, Pallas kernels for 0% -> 0%
where the time goes in v1:
time: 551 us; the launch traced here: 545 us
  waiting for transfers between devices  121 us (22%)
  local copies, waits for them, and re-layouts  114 us (21%)
  other arithmetic  95.4 us (17%)
  starting transfers between devices  75.6 us (14%)
  matrix products  74.2 us (13%)
  blocking collectives  48 us (9%)
  between operations  15.1 us (3%)
    gather x2, local copies, waits for them, and re-layouts, on_device(): conv_segment[window_index] == conv_segment[HALF:HALF + conv_rows][:, None]  55.6 us
    psum x1, blocking collectives, on_device(): kernel_sum, gain_sum = lax.psum((kernel_terms, gain_terms), ('head', 'tm'))  48 us
    all_gather x1, waiting for transfers between devices, on_device(): lax.all_gather(qkv_proj, 'tm', axis=0, tiled=True)  46.5 us
    psum x1, waiting for transfers between devices, on_device(): kernel_sum, gain_sum = lax.psum((kernel_terms, gain_terms), ('head', 'tm'))  42.5 us
    ppermute x8, waiting for transfers between devices, draft_strings(): high = ppermute(high, 'tm', pile)  29.1 us
    reduce_sum x6, other arithmetic, on_device(): jnp.sum(depth_float * gated_padded[offset:offset + conv_rows].astype(jnp....  27.5 us
    dot_general x2, matrix products, attend(): jnp.einsum('qhd,khd->hqk', query_rows, key_part, preferred_element_type=j...  26 us
    ppermute x7, starting transfers between devices, draft_strings(): u1 = ppermute(u1, 'tm', inbox)  24.6 us
  transfers between devices with their start and end apart: 33, of which 11 were waited for; matrix products, arithmetic and copies ran while one was open for 45% of the time, Pallas kernels for 0%

profile of v1, /device:TPU:0, one launch (start us, length us, event | category | flops | bytes accessed | tf_op | source)
XLA Modules:
  0.0 544.6 jit_solution(1991582526244077929)
XLA Ops:
  11.9 46.5 %all-gather.4.cloned.1.call-done = bf16[1024,3,512]{2,0,1:T(8,128)(2,1)} async-done(((bf16[64,3,512]{2,0,1:T(8,128)(2,1)}), bf16[1024,3,512]{2,0,1:T(8,128)(2,1)}) %all-gather.4.cloned.1.call-update) | async-done | bytes 3145744 | tf_op jit(solution)/shard_map/all_gather | solution.py:85
  58.5 4.7 copy.43
  63.2 5.4 fusion.83
  68.8 2.4 copy-done.14
  77.2 4.7 fusion.246
  84.7 4.2 collective-permute-start
  93.1 3.4 pad_maximum_fusion
  96.5 65.4 %while.12 = (s32[]{:T(128)}, bf16[2,512,512]{2,1,0:T(8,128)(2,1)}, s32[2]{0:T(128)S(1)}, bf16[2048,2,512]{2,0,1:T(8,128)(2,1)}, s32[2048]{0:T(1024)S(1)}, /*inde...) while((s32[]{:T(128)}, bf16[2,512,512]{2,1,0:T(8,128)(2,1)}, ...), condition=%wide.region_8.9_spmd, body=%wide.region_6.8_spmd.sunk | while | flops 1655697408 | bytes 89448936 | solution.py:170
  103.7 13.0 %fusion.267 = (f32[8,512]{1,0:T(8,128)S(1)}, f32[8,512,1536]{2,1,0:T(8,128)}) fusion(f32[8]{0:T(128)S(1)} %bitcast.240, pred[512,1536]{1,0:T(8,128)(4,1)} %broadcast_compare_fusion.2, bf16[1536,8,64]{0,2,1:T(8,128)(2,1)S(1)} %bitcast.131, bf16[1024,8,64]{0,2,1:T(8,128)(2,1)} %get-tuple-element.344, s32[]{:T(128)S(6)} %select_n.250), kind=kOutput, calls=%fused_computation.3.clone.1 | convolution fusion | flops 824176640 | bytes 28065828 | tf_op jit(solution)/shard_map/while/body/eval_jaxpr/qhd,khd->hqk/dot_general | solution.py:155
  116.7 11.2 %fusion.268 = bf16[8,64,512]{2,1,0:T(8,128)(2,1)S(1)} fusion(bf16[1536,8,64]{0,2,1:T(8,128)(2,1)S(1)} %bitcast.130, f32[8,512,1536]{2,1,0:T(8,128)} %get-tuple-element.307, f32[8,512]{1,0:T(8,128)S(1)} %get-tuple-element.308, f32[8]{0:T(128)S(1)} %bitcast.241, pred[512,1536]{1,0:T(8,128)(4,1)S(1)} %copy-done.5), kind=kOutput, calls=%fused_computation.6.clone.1 | convolution fusion | flops 830734336 | bytes 28065824 | tf_op jit(solution)/shard_map/while/body/eval_jaxpr/hqk,khd->qhd/dot_general | solution.py:160
  136.4 13.0 %fusion.267 = (f32[8,512]{1,0:T(8,128)S(1)}, f32[8,512,1536]{2,1,0:T(8,128)}) fusion(f32[8]{0:T(128)S(1)} %bitcast.240, pred[512,1536]{1,0:T(8,128)(4,1)} %broadcast_compare_fusion.2, bf16[1536,8,64]{0,2,1:T(8,128)(2,1)S(1)} %bitcast.131, bf16[1024,8,64]{0,2,1:T(8,128)(2,1)} %get-tuple-element.344, s32[]{:T(128)S(6)} %select_n.250), kind=kOutput, calls=%fused_computation.3.clone.1 | convolution fusion | flops 824176640 | bytes 28065828 | tf_op jit(solution)/shard_map/while/body/eval_jaxpr/qhd,khd->hqk/dot_general | solution.py:155
  149.4 11.2 %fusion.268 = bf16[8,64,512]{2,1,0:T(8,128)(2,1)S(1)} fusion(bf16[1536,8,64]{0,2,1:T(8,128)(2,1)S(1)} %bitcast.130, f32[8,512,1536]{2,1,0:T(8,128)} %get-tuple-element.307, f32[8,512]{1,0:T(8,128)S(1)} %get-tuple-element.308, f32[8]{0:T(128)S(1)} %bitcast.241, pred[512,1536]{1,0:T(8,128)(4,1)S(1)} %copy-done.5), kind=kOutput, calls=%fused_computation.6.clone.1 | convolution fusion | flops 830734336 | bytes 28065824 | tf_op jit(solution)/shard_map/while/body/eval_jaxpr/hqk,khd->qhd/dot_general | solution.py:160
  161.9 4.1 convolution_convert_fusion
  167.0 18.4 %collective-permute-start.2 = (bf16[64,2048]{1,0:T(8,128)(2,1)S(1)}, bf16[64,2048]{1,0:T(8,128)(2,1)S(1)}, u32[]{:S(2)}, u32[]{:S(2)}) collective-permute-start(bf16[64,2048]{1,0:T(8,128)(2,1)S(1)} %copy-done.16), channel_id=1, source_target_pairs={{0,1},{1,2},{2,3},{3,4},{4,5},{5,6},{6,7},{7,8},{8,9},{9,10},{10,1... | collective-permute-start | bytes 786440 | tf_op jit(solution)/shard_map/ppermute | solution.py:105
  185.4 3.6 all-to-all-start.1
  190.2 2.5 broadcast_in_dim.47
  193.4 2.4 convert_element_type.293
  195.9 55.4 %gather_fusion = s32[15872]{0:T(1024)S(1)} fusion(s32[542]{0:T(1024)S(1)} %compare_select_fusion.2, s32[16384]{0:T(1024)S(1)} %pad_clamp_fusion), kind=kCustom, calls=%fused_computation | custom fusion | bytes 190464 | tf_op jit(solution)/shard_map/gather | solution.py:202
  251.8 2.6 collective-permute-start.4
  257.7 6.9 %collective-permute-done.4 = bf16[64,2048]{1,0:T(8,128)(2,1)S(1)} collective-permute-done((bf16[64,2048]{1,0:T(8,128)(2,1)S(1)}, bf16[64,2048]{1,0:T(8,128)(2,1)S(1)}, u32[]{:S(2)}, u32[]{:S(2)}) %collective-permute-start.4) | collective-permute-done | bytes 262176 | tf_op jit(solution)/shard_map/ppermute | solution.py:105
  264.6 4.4 collective-permute-start.7
  270.5 5.4 collective-permute-done.6
  275.9 4.4 collective-permute-start.9
  281.8 2.6 collective-permute-done.8
  284.4 4.5 collective-permute-start.11
  290.4 2.5 collective-permute-done.10
  292.9 4.6 collective-permute-start.13
  299.0 2.4 collective-permute-done.12
  301.5 4.7 collective-permute-start.15
  311.4 7.0 %collective-permute-done.16 = bf16[64,2048]{1,0:T(8,128)(2,1)S(1)} collective-permute-done((bf16[64,2048]{1,0:T(8,128)(2,1)S(1)}, bf16[64,2048]{1,0:T(8,128)(2,1)S(1)}, u32[]{:S(2)}, u32[]{:S(2)}) %collective-permute-start.16) | collective-permute-done | bytes 262176 | tf_op jit(solution)/shard_map/ppermute | solution.py:105
  321.8 4.6 fusion.176
  330.7 2.6 slice_reduce_fusion.30
  337.6 3.4 collective-permute-start.18
  341.4 18.6 %fusion.244 = (f32[512]{0:T(512)S(1)}, f32[512,1024]{1,0:T(8,128)S(1)}) fusion(f32[512]{0:T(512)S(1)} %get-tuple-element.160, bf16[15,1024]{1,0:T(8,128)(2,1)S(1)} %broadcast_select_fusion.1, bf16[512,1024]{1,0:T(8,128)(2,1)S(1)} %multiply_convert_fusion.6, f32[1024]{0:T(1024)S(1)} %bitcast.163, f32[512]{0:T(512)S(1)} %get-tuple-element.161, ...), kind=kLoop, calls=%fused_computation.499 | loop fusion | flops 112197120 | bytes 3399680 | tf_op jit(solution)/shard_map/reduce_sum | solution.py:34
  360.5 5.0 multiply_reduce_fusion.1
  365.6 7.3 %fusion.160 = (f32[1024]{0:T(1024)}, f32[1024]{0:T(1024)}, f32[1024]{0:T(1024)}, f32[1024]{0:T(1024)}, f32[1024]{0:T(1024)}, /*index=5*/f32[1024]{0:T(1024)}, bf16[512,1024]{1,0:T(8,128)(2,1)S(1)}) fusion(f32[512]{0:T(512)S(1)} %get-tuple-element.161, bf16[15,1024]{1,0:T(8,128)(2,1)S(1)} %broadcast_select_fusion.1, ...), kind=kLoop, calls=%fused_computation.293 | loop fusion | flops 26732544 | bytes 6371328 | tf_op jit(solution)/shard_map/reduce_sum | solution.py:233
  372.9 4.2 fusion.128
  377.1 3.7 fusion.130
  380.8 7.1 %fusion.162 = (f32[1024]{0:T(1024)}, f32[1024]{0:T(1024)}, f32[1024]{0:T(1024)}, f32[1024]{0:T(1024)}, f32[1024]{0:T(1024)}, /*index=5*/f32[1024]{0:T(1024)}) fusion(bf16[512,1024]{1,0:T(8,128)(2,1)S(1)} %get-tuple-element.204, bf16[15,1024]{1,0:T(8,128)(2,1)S(1)} %broadcast_select_fusion.1, bf16[512,1024]{1,0:T(8,128)(2,1)S(1)} %multiply_convert_fusion.6, ...), kind=kLoop, calls=%fused_computation.295 | loop fusion | flops 22538240 | bytes 2164736 | tf_op jit(solution)/shard_map/reduce_sum | solution.py:233
  391.5 3.2 fusion.158
  399.1 3.6 all-to-all-start
  402.9 5.5 %stack.144 = f32[31,1024]{1,0:T(8,128)} concatenate(f32[1,1024]{1,0:T(1,128)} %bitcast.216, f32[1,1024]{1,0:T(1,128)} %bitcast.235, f32[1,1024]{1,0:T(1,128)} %bitcast.234, f32[1,1024]{1,0:T(1,128)} %bitcast.233, f32[1,1024]{1,0:T(1,128)} %bitcast.218, f32[1,1024]{1,0:T(1,128)} %bitcast.219, f32[1,1024]{1,0:T(1,128)} %bitcast.220, f32[1,1024]{1,0:T(1,128)} %bitcast.221, ...), dimensions={0} | concatenate | bytes 253952 | tf_op jit(solution)/shard_map/stack | solution.py:231
  408.4 3.0 collective-permute-start.22
  412.3 19.3 %multiply_convert_fusion.3 = (bf16[512,1024]{1,0:T(8,128)(2,1)S(1)}, f32[512,1024]{1,0:T(8,128)S(1)}) fusion(f32[512,2048]{1,0:T(8,128)} %copy-done.3, f32[512]{0:T(512)S(1)} %get-tuple-element.160, bf16[15,1024]{1,0:T(8,128)(2,1)S(1)} %broadcast_select_fusion, bf16[512,1024]{1,0:T(8,128)(2,1)S(1)} %get-tuple-element.204, f32[1024]{0:T(1024)S(1)} %bitcast.168, ...), kind=kLoop, calls=%fused_computation.310 | loop fusion | flops 114294784 | bytes 6543360 | tf_op jit(solution)/shard_map/convert
  432.5 5.1 fusion.19
  439.5 3.6 all-to-all-start.2
  443.2 48.0 %psum.15 = f32[2,1024]{1,0:T(2,128)S(1)} all-reduce(f32[2,1024]{1,0:T(2,128)S(1)} %pad_maximum_fusion.6), channel_id=1, replica_groups=mesh['head'=2,'tm'=16] {'head','tm'}, use_global_device_ids=true, to_apply=%region_53.54 | all-reduce | flops 2048 | bytes 16384 | tf_op jit(solution)/shard_map/psum | solution.py:253
  491.8 42.5 %all-reduce.2.cloned.1.call-done = f32[31,1024]{1,0:T(8,128)} async-done(((f32[31,1024]{1,0:T(8,128)}), f32[31,1024]{1,0:T(8,128)}) %all-reduce.2.cloned.1.call-update) | async-done | bytes 126992 | tf_op jit(solution)/shard_map/psum | solution.py:253
  (260 shorter events, 79.2 us)
Async XLA Ops:
  7.2 51.3 %all-gather.4.cloned.1.call-start = ((), (), s32[]{:S(2)}) async-start(), calls=%async_computation.4 | async-start | bytes 3342336 | tf_op jit(solution)/shard_map/all_gather | solution.py:85
  7.9 154.0 %all-gather.6.cloned.1.call-start = ((), (), s32[]{:S(2)}) async-start(), calls=%async_computation.5 | async-start | bytes 1114112 | tf_op jit(solution)/shard_map/all_gather | solution.py:86
  8.7 310.4 %reduce-scatter.2.cloned.1.call-start = ((), (), s32[]{:S(2)}) async-start(), calls=%async_computation.6 | async-start | bytes 3145728 | tf_op jit(solution)/shard_map/reduce_scatter | solution.py:173
  11.9 77.0 %copy-start.38 = (s32[128]{0:T(128)}, s32[128]{0:T(128)S(1)}, u32[]{:S(2)}) copy-start(s32[128]{0:T(128)S(1)} %reduce) | copy-start | bytes 1540
  11.9 51.2 %copy-start.49 = (f32[1024]{0:T(1024)S(1)}, f32[1024]{0:T(1024)}, u32[]{:S(2)}) copy-start(f32[1024]{0:T(1024)} %param.16) | copy-start | bytes 12292
  83.4 9.7 %collective-permute-start.1 = (bf16[512,2,512]{2,0,1:T(8,128)(2,1)}, bf16[512,2,512]{2,0,1:T(8,128)(2,1)}, u32[]{:S(2)}, u32[]{:S(2)}) collective-permute-start(bf16[512,2,512]{2,0,1:T(8,128)(2,1)} %get-tuple-element.218), channel_id=1, source_target_pairs={{1,0},{2,1},{3,2},{4,3},{5,4},{6,5},{7,6},{8,7},{9,8},{10,9},{11,1... | collective-permute-start | bytes 3145736 | tf_op jit(solution)/shard_map/ppermute | solution.py:26
  84.7 8.4 %collective-permute-start = (bf16[512,2,512]{2,0,1:T(8,128)(2,1)}, bf16[512,2,512]{2,0,1:T(8,128)(2,1)}, u32[]{:S(2)}, u32[]{:S(2)}) collective-permute-start(bf16[512,2,512]{2,0,1:T(8,128)(2,1)} %get-tuple-element.217), channel_id=1, source_target_pairs={{0,1},{1,2},{2,3},{3,4},{4,5},{5,6},{6,7},{7,8},{8,9},{9,10},{10,1... | collective-permute-start | bytes 3145736 | tf_op jit(solution)/shard_map/ppermute | solution.py:24
  103.7 13.0 %copy-start.2 = (bf16[1536,1,512]{0,2,1:T(8,128)(2,1)S(1)}, bf16[1536,1,512]{0,2,1:T(8,128)(2,1)}, u32[]{:S(2)}) copy-start(bf16[1536,1,512]{0,2,1:T(8,128)(2,1)} %copy.68) | copy-start | bytes 4718596 | tf_op jit(solution)/shard_map/while
  103.7 13.0 %copy-start.5 = (pred[512,1536]{1,0:T(8,128)(4,1)S(1)}, pred[512,1536]{1,0:T(8,128)(4,1)}, u32[]{:S(2)}) copy-start(pred[512,1536]{1,0:T(8,128)(4,1)} %broadcast_compare_fusion.2) | copy-start | bytes 2359300 | tf_op jit(solution)/shard_map/while
  136.4 13.0 %copy-start.2 = (bf16[1536,1,512]{0,2,1:T(8,128)(2,1)S(1)}, bf16[1536,1,512]{0,2,1:T(8,128)(2,1)}, u32[]{:S(2)}) copy-start(bf16[1536,1,512]{0,2,1:T(8,128)(2,1)} %copy.68) | copy-start | bytes 4718596 | tf_op jit(solution)/shard_map/while
  136.4 13.0 %copy-start.5 = (pred[512,1536]{1,0:T(8,128)(4,1)S(1)}, pred[512,1536]{1,0:T(8,128)(4,1)}, u32[]{:S(2)}) copy-start(pred[512,1536]{1,0:T(8,128)(4,1)} %broadcast_compare_fusion.2) | copy-start | bytes 2359300 | tf_op jit(solution)/shard_map/while
  166.1 23.5 %copy-start.17 = (f32[31,1024]{1,0:T(8,128)S(1)}, f32[31,1024]{1,0:T(8,128)}, u32[]{:S(2)}) copy-start(f32[31,1024]{1,0:T(8,128)} %param.22) | copy-start | bytes 380932
  166.1 23.6 %copy-start.39 = (s32[128]{0:T(128)S(1)}, s32[128]{0:T(128)}, u32[]{:S(2)}) copy-start(s32[128]{0:T(128)} %copy-done.38) | copy-start | bytes 1540
  167.0 84.8 %collective-permute-start.2 = (bf16[64,2048]{1,0:T(8,128)(2,1)S(1)}, bf16[64,2048]{1,0:T(8,128)(2,1)S(1)}, u32[]{:S(2)}, u32[]{:S(2)}) collective-permute-start(bf16[64,2048]{1,0:T(8,128)(2,1)S(1)} %copy-done.16), channel_id=1, source_target_pairs={{0,1},{1,2},{2,3},{3,4},{4,5},{5,6},{6,7},{7,8},{8,9},{9,10},{10,1... | collective-permute-start | bytes 786440 | tf_op jit(solution)/shard_map/ppermute | solution.py:105
  185.4 69.0 %collective-permute-start.3 = (bf16[64,2048]{1,0:T(8,128)(2,1)S(1)}, bf16[64,2048]{1,0:T(8,128)(2,1)S(1)}, u32[]{:S(2)}, u32[]{:S(2)}) collective-permute-start(bf16[64,2048]{1,0:T(8,128)(2,1)S(1)} %copy-done.16), channel_id=1, source_target_pairs={{0,15},{1,0},{2,1},{3,2},{4,3},{5,4},{6,5},{7,6},{8,7},{9,8},{10,9... | collective-permute-start | bytes 786440 | tf_op jit(solution)/shard_map/ppermute | solution.py:115
  185.4 151.1 %all-to-all-start.1 = ((bf16[2,512,512]{2,1,0:T(8,128)(2,1)}), bf16[2,512,512]{2,1,0:T(8,128)(2,1)S(1)}, u32[]{:S(2)}, u32[]{:S(2)}) async-start(bf16[2,512,512]{2,1,0:T(8,128)(2,1)} %bitcast.48), calls=%async_computation.2 | async-start | bytes 2097152 | tf_op jit(solution)/shard_map/all_to_all | solution.py:225
  188.9 171.6 %all-gather.8.cloned.1.call-start = ((), (), s32[]{:S(2)}) async-start(), calls=%async_computation.7 | async-start | bytes 2228224 | tf_op jit(solution)/shard_map/all_gather | solution.py:124
  251.8 12.9 %collective-permute-start.4 = (bf16[64,2048]{1,0:T(8,128)(2,1)S(1)}, bf16[64,2048]{1,0:T(8,128)(2,1)S(1)}, u32[]{:S(2)}, u32[]{:S(2)}) collective-permute-start(bf16[64,2048]{1,0:T(8,128)(2,1)S(1)} %collective-permute-done.2), channel_id=1, source_target_pairs={{0,1},{1,2},{2,3},{3,4},{4,5},{5,6},{6,7},{7,8},{8,9},{9,10},{10,1... | collective-permute-start | bytes 786440 | tf_op jit(solution)/shard_map/ppermute | solution.py:105
  254.4 10.2 %collective-permute-start.5 = (bf16[64,2048]{1,0:T(8,128)(2,1)S(1)}, bf16[64,2048]{1,0:T(8,128)(2,1)S(1)}, u32[]{:S(2)}, u32[]{:S(2)}) collective-permute-start(bf16[64,2048]{1,0:T(8,128)(2,1)S(1)} %collective-permute-done.3), channel_id=1, source_target_pairs={{0,15},{1,0},{2,1},{3,2},{4,3},{5,4},{6,5},{7,6},{8,7},{9,8},{10,9... | collective-permute-start | bytes 786440 | tf_op jit(solution)/shard_map/ppermute | solution.py:115
  264.6 11.3 %collective-permute-start.6 = (bf16[64,2048]{1,0:T(8,128)(2,1)S(1)}, bf16[64,2048]{1,0:T(8,128)(2,1)S(1)}, u32[]{:S(2)}, u32[]{:S(2)}) collective-permute-start(bf16[64,2048]{1,0:T(8,128)(2,1)S(1)} %collective-permute-done.4), channel_id=1, source_target_pairs={{0,1},{1,2},{2,3},{3,4},{4,5},{5,6},{6,7},{7,8},{8,9},{9,10},{10,1... | collective-permute-start | bytes 786440 | tf_op jit(solution)/shard_map/ppermute | solution.py:105
  264.6 11.3 %collective-permute-start.7 = (bf16[64,2048]{1,0:T(8,128)(2,1)S(1)}, bf16[64,2048]{1,0:T(8,128)(2,1)S(1)}, u32[]{:S(2)}, u32[]{:S(2)}) collective-permute-start(bf16[64,2048]{1,0:T(8,128)(2,1)S(1)} %collective-permute-done.5), channel_id=1, source_target_pairs={{0,15},{1,0},{2,1},{3,2},{4,3},{5,4},{6,5},{7,6},{8,7},{9,8},{10,9... | collective-permute-start | bytes 786440 | tf_op jit(solution)/shard_map/ppermute | solution.py:115
  275.9 8.5 %collective-permute-start.8 = (bf16[64,2048]{1,0:T(8,128)(2,1)S(1)}, bf16[64,2048]{1,0:T(8,128)(2,1)S(1)}, u32[]{:S(2)}, u32[]{:S(2)}) collective-permute-start(bf16[64,2048]{1,0:T(8,128)(2,1)S(1)} %collective-permute-done.6), channel_id=1, source_target_pairs={{0,1},{1,2},{2,3},{3,4},{4,5},{5,6},{6,7},{7,8},{8,9},{9,10},{10,1... | collective-permute-start | bytes 786440 | tf_op jit(solution)/shard_map/ppermute | solution.py:105
  275.9 8.5 %collective-permute-start.9 = (bf16[64,2048]{1,0:T(8,128)(2,1)S(1)}, bf16[64,2048]{1,0:T(8,128)(2,1)S(1)}, u32[]{:S(2)}, u32[]{:S(2)}) collective-permute-start(bf16[64,2048]{1,0:T(8,128)(2,1)S(1)} %collective-permute-done.7), channel_id=1, source_target_pairs={{0,15},{1,0},{2,1},{3,2},{4,3},{5,4},{6,5},{7,6},{8,7},{9,8},{10,9... | collective-permute-start | bytes 786440 | tf_op jit(solution)/shard_map/ppermute | solution.py:115
  284.4 8.5 %collective-permute-start.10 = (bf16[64,2048]{1,0:T(8,128)(2,1)S(1)}, bf16[64,2048]{1,0:T(8,128)(2,1)S(1)}, u32[]{:S(2)}, u32[]{:S(2)}) collective-permute-start(bf16[64,2048]{1,0:T(8,128)(2,1)S(1)} %collective-permute-done.8), channel_id=1, source_target_pairs={{0,1},{1,2},{2,3},{3,4},{4,5},{5,6},{6,7},{7,8},{8,9},{9,10},{10,1... | collective-permute-start | bytes 786440 | tf_op jit(solution)/shard_map/ppermute | solution.py:105
  284.4 8.5 %collective-permute-start.11 = (bf16[64,2048]{1,0:T(8,128)(2,1)S(1)}, bf16[64,2048]{1,0:T(8,128)(2,1)S(1)}, u32[]{:S(2)}, u32[]{:S(2)}) collective-permute-start(bf16[64,2048]{1,0:T(8,128)(2,1)S(1)} %collective-permute-done.9), channel_id=1, source_target_pairs={{0,15},{1,0},{2,1},{3,2},{4,3},{5,4},{6,5},{7,6},{8,7},{9,8},{10,9... | collective-permute-start | bytes 786440 | tf_op jit(solution)/shard_map/ppermute | solution.py:115
  292.9 8.5 %collective-permute-start.12 = (bf16[64,2048]{1,0:T(8,128)(2,1)S(1)}, bf16[64,2048]{1,0:T(8,128)(2,1)S(1)}, u32[]{:S(2)}, u32[]{:S(2)}) collective-permute-start(bf16[64,2048]{1,0:T(8,128)(2,1)S(1)} %collective-permute-done.10), channel_id=1, source_target_pairs={{0,1},{1,2},{2,3},{3,4},{4,5},{5,6},{6,7},{7,8},{8,9},{9,10},{10,1... | collective-permute-start | bytes 786440 | tf_op jit(solution)/shard_map/ppermute | solution.py:105
  292.9 8.5 %collective-permute-start.13 = (bf16[64,2048]{1,0:T(8,128)(2,1)S(1)}, bf16[64,2048]{1,0:T(8,128)(2,1)S(1)}, u32[]{:S(2)}, u32[]{:S(2)}) collective-permute-start(bf16[64,2048]{1,0:T(8,128)(2,1)S(1)} %collective-permute-done.11), channel_id=1, source_target_pairs={{0,15},{1,0},{2,1},{3,2},{4,3},{5,4},{6,5},{7,6},{8,7},{9,8},{10,9... | collective-permute-start | bytes 786440 | tf_op jit(solution)/shard_map/ppermute | solution.py:115
  301.4 8.5 %collective-permute-start.14 = (bf16[64,2048]{1,0:T(8,128)(2,1)S(1)}, bf16[64,2048]{1,0:T(8,128)(2,1)S(1)}, u32[]{:S(2)}, u32[]{:S(2)}) collective-permute-start(bf16[64,2048]{1,0:T(8,128)(2,1)S(1)} %collective-permute-done.12), channel_id=1, source_target_pairs={{0,1},{1,2},{2,3},{3,4},{4,5},{5,6},{6,7},{7,8},{8,9},{9,10},{10,1... | collective-permute-start | bytes 786440 | tf_op jit(solution)/shard_map/ppermute | solution.py:105
  301.5 9.2 %collective-permute-start.15 = (bf16[64,2048]{1,0:T(8,128)(2,1)S(1)}, bf16[64,2048]{1,0:T(8,128)(2,1)S(1)}, u32[]{:S(2)}, u32[]{:S(2)}) collective-permute-start(bf16[64,2048]{1,0:T(8,128)(2,1)S(1)} %collective-permute-done.13), channel_id=1, source_target_pairs={{0,15},{1,0},{2,1},{3,2},{4,3},{5,4},{6,5},{7,6},{8,7},{9,8},{10,9... | collective-permute-start | bytes 786440 | tf_op jit(solution)/shard_map/ppermute | solution.py:115
  309.9 8.5 %collective-permute-start.16 = (bf16[64,2048]{1,0:T(8,128)(2,1)S(1)}, bf16[64,2048]{1,0:T(8,128)(2,1)S(1)}, u32[]{:S(2)}, u32[]{:S(2)}) collective-permute-start(bf16[64,2048]{1,0:T(8,128)(2,1)S(1)} %collective-permute-done.14), channel_id=1, source_target_pairs={{0,1},{1,2},{2,3},{3,4},{4,5},{5,6},{6,7},{7,8},{8,9},{9,10},{10,1... | collective-permute-start | bytes 786440 | tf_op jit(solution)/shard_map/ppermute | solution.py:105
  328.5 4.9 collective-permute-start.19
  333.3 4.3 collective-permute-start.17
  333.4 7.6 %collective-permute-start.20 = (bf16[15,1024]{1,0:T(8,128)(2,1)S(1)}, bf16[15,1024]{1,0:T(8,128)(2,1)S(1)}, u32[]{:S(2)}, u32[]{:S(2)}) collective-permute-start(bf16[15,1024]{1,0:T(8,128)(2,1)S(1)} %collective-permute-done.19), channel_id=1, source_target_pairs={{1,0},{2,1},{3,2},{4,3},{5,4},{6,5},{7,6},{8,7},{9,8},{10,9},{11,1... | collective-permute-start | bytes 92168 | tf_op jit(solution)/shard_map/ppermute | solution.py:26
  336.4 23.7 %copy-start.18 = (f32[512]{0:T(512)}, f32[512]{0:T(512)S(1)}, u32[]{:S(2)}) copy-start(f32[512]{0:T(512)S(1)} %get-tuple-element.186) | copy-start | bytes 6148
  336.4 23.7 %copy-start.20 = (f32[512]{0:T(512)}, f32[512]{0:T(512)S(1)}, u32[]{:S(2)}) copy-start(f32[512]{0:T(512)S(1)} %get-tuple-element.187) | copy-start | bytes 6148
  337.6 3.9 collective-permute-start.18
  341.4 19.1 %copy-start.40 = (f32[1024]{0:T(1024)S(1)}, f32[1024]{0:T(1024)}, u32[]{:S(2)}) copy-start(f32[1024]{0:T(1024)} %param.23) | copy-start | bytes 12292
  372.9 17.0 %copy-start.46 = (bf16[1024,1024]{1,0:T(8,128)(2,1)S(1)}, bf16[1024,1024]{1,0:T(8,128)(2,1)}, u32[]{:S(2)}) copy-start(bf16[1024,1024]{1,0:T(8,128)(2,1)} %all-gather.8.cloned.1.call-done) | copy-start | bytes 6291460
  377.1 12.8 %copy-start.9 = (f32[512,1024]{1,0:T(8,128)S(1)}, f32[512,1024]{1,0:T(8,128)}, u32[]{:S(2)}) copy-start(f32[512,1024]{1,0:T(8,128)} %copy-done.8) | copy-start | bytes 6291460
  377.1 12.8 %copy-start.11 = (bf16[512,1024]{1,0:T(8,128)(2,1)S(1)}, bf16[512,1024]{1,0:T(8,128)(2,1)}, u32[]{:S(2)}) copy-start(bf16[512,1024]{1,0:T(8,128)(2,1)} %copy-done.10) | copy-start | bytes 3145732
  387.9 6.8 %collective-permute-start.23 = (bf16[15,1024]{1,0:T(8,128)(2,1)S(1)}, bf16[15,1024]{1,0:T(8,128)(2,1)S(1)}, u32[]{:S(2)}, u32[]{:S(2)}) collective-permute-start(bf16[15,1024]{1,0:T(8,128)(2,1)S(1)} %get-tuple-element.220), channel_id=1, source_target_pairs={{16,0},{0,16},{17,1},{1,17},{18,2},{2,18},{19,3},{3,19},{20,4},{4,... | collective-permute-start | bytes 92168 | tf_op jit(solution)/shard_map/ppermute | solution.py:26
  389.9 18.5 %collective-permute-start.21 = (bf16[15,1024]{1,0:T(8,128)(2,1)S(1)}, bf16[15,1024]{1,0:T(8,128)(2,1)S(1)}, u32[]{:S(2)}, u32[]{:S(2)}) collective-permute-start(bf16[15,1024]{1,0:T(8,128)(2,1)S(1)} %get-tuple-element.219), channel_id=1, source_target_pairs={{0,16},{16,0},{1,17},{17,1},{2,18},{18,2},{3,19},{19,3},{4,20},{20... | collective-permute-start | bytes 92168 | tf_op jit(solution)/shard_map/ppermute | solution.py:24
  394.7 16.8 %collective-permute-start.24 = (bf16[15,1024]{1,0:T(8,128)(2,1)S(1)}, bf16[15,1024]{1,0:T(8,128)(2,1)S(1)}, u32[]{:S(2)}, u32[]{:S(2)}) collective-permute-start(bf16[15,1024]{1,0:T(8,128)(2,1)S(1)} %collective-permute-done.23), channel_id=1, source_target_pairs={{1,0},{2,1},{3,2},{4,3},{5,4},{6,5},{7,6},{8,7},{9,8},{10,9},{11,1... | collective-permute-start | bytes 92168 | tf_op jit(solution)/shard_map/ppermute | solution.py:26
  399.1 40.4 %all-to-all-start = ((bf16[512,2,512]{2,0,1:T(8,128)(2,1)}), bf16[512,2,512]{2,0,1:T(8,128)(2,1)S(1)}, u32[]{:S(2)}, u32[]{:S(2)}) async-start(bf16[512,2,512]{2,0,1:T(8,128)(2,1)} %bitcast.136), calls=%async_computation.1 | async-start | bytes 2097152 | tf_op jit(solution)/shard_map/all_to_all | solution.py:224
  402.7 131.6 %all-reduce.2.cloned.1.call-start = ((), (), s32[]{:S(2)}) async-start(), calls=%async_computation.8 | async-start | bytes 262144 | tf_op jit(solution)/shard_map/psum | solution.py:253
  408.4 3.9 collective-permute-start.22
  412.3 19.3 %copy-start.4 = (f32[512,2048]{1,0:T(8,128)S(1)}, f32[512,2048]{1,0:T(8,128)}, u32[]{:S(2)}) copy-start(f32[512,2048]{1,0:T(8,128)} %copy-done.3) | copy-start | bytes 12582916
  439.5 96.4 %all-to-all-start.2 = ((bf16[512,2,512]{2,0,1:T(8,128)(2,1)}), bf16[512,2,512]{2,0,1:T(8,128)(2,1)S(1)}, u32[]{:S(2)}, u32[]{:S(2)}) async-start(bf16[512,2,512]{2,0,1:T(8,128)(2,1)} %bitcast.114), calls=%async_computation.3 | async-start | bytes 2097152 | tf_op jit(solution)/shard_map/all_to_all | solution.py:255
  (40 other events, 188.7 us)
Sparse Core Ops, SparseCore 0:
  10.2 48.2 all-gather.3
  61.2 36.6 all-gather.5
  166.2 61.4 reduce-scatter.1
  229.7 44.7 all-gather.7
  409.3 124.9 all-reduce.1
